TPU v7x, 32 devices: a whole 2x2x4 slice. The times are simulated.
32 devices in a mesh: groups: 2 (over y), space: 4 (over z), clus: 4 (over x, core).
Axes of the slice: x: 2, y: 2, z: 4, core: 2. Of those that a mesh axis runs over, the one named last changes fastest.
Arguments:
- snapshots: bfloat16 [256, 5, 49152], P('groups', None, ('space', 'clus')), parts along dimension 0
- labels: int32 [256], P('groups'), parts along dimension 0, may hold values from 0 to 3, as said below
- start: float32 [256, 16], P('groups'), parts along dimension 0, may hold values from -6 to 6
- successor: int32 [8], P('groups'), parts along dimension 0, may hold values from 0 to 3, as said below
Outputs:
- modes: bfloat16 [8, 16, 5, 49152], P(('groups', 'clus'), None, None, 'space'), parts along dimension 0
- coefficients: float32 [256, 16], P(('groups', 'clus')), parts along dimension 0
- correlations: float32 [8, 16, 16], P(('groups', 'clus')), parts along dimension 0
There are 2 independent parts, one for each index of `groups`. A program takes and returns all parts, laid end to end along the dimension named above; each array names one. Nothing has to cross between parts.
Inputs may be any that keep to these rules, and one draw needn't show every extreme that they name: `labels`: of the 32 snapshots of each aligned block (those of one index of clus), every cluster holds at least 6 and at most 8; in every block some cluster holds exactly 8. Following successor from any cluster visits all 4 clusters once before returning.
All inputs are finite; a program needn't handle non-finite values.
Results may differ from a plain program's by a relative error of at most 0.0045.
Values may be sent and summed in bfloat16 or wider, within the bound.
No kernel may reach another device: no remote copies, remote signals or barrier semaphores. Data moves between devices by JAX's collectives and lax.ppermute only.
A program may use at most 64 MiB of HBM per device.

v0:
```python
import jax
import jax.numpy as jnp
from jax import lax
from jax.sharding import PartitionSpec as P

ITERS = 2


def subspace(gram, member, start):
    basis = member[:, :, None] * start[None, :, :]
    for step in range(ITERS):
        image = (
            member[:, :, None]
            * jnp.einsum("st,ktm->ksm", gram, basis, precision=lax.Precision.HIGHEST)
            + basis
        )
        inner = jnp.einsum("ksm,ksn->kmn", image, image, precision=lax.Precision.HIGHEST)
        lower = jnp.linalg.cholesky(inner)
        basis = lax.linalg.triangular_solve(
            lower, image, left_side=False, lower=True, transpose_a=True
        )
    return basis


def local(snapshots, labels, start, successor):
    count, variables, cells = snapshots.shape
    clusters = lax.axis_size("clus")
    owner = lax.axis_index("clus")
    total_rows = variables * cells * lax.axis_size("space") * clusters
    flat = snapshots.reshape(count, variables * cells)
    partial_value = lax.dot_general(
        flat, flat, (((1,), (1,)), ((), ())), preferred_element_type=jnp.float32
    )
    gram = lax.psum(partial_value, ("space", "clus")) / total_rows
    cluster_ids = jnp.arange(clusters, dtype=jnp.int32)
    member = (labels[None, :] == cluster_ids[:, None]).astype(jnp.float32)
    basis = subspace(gram, member, start)
    picked = jnp.einsum("ks,ksm->sm", member, basis, precision=lax.Precision.HIGHEST)
    snap_dev = count // clusters
    coefficients = lax.dynamic_slice_in_dim(picked, owner * snap_dev, snap_dev, 0)
    rounded = basis.astype(jnp.bfloat16)
    mode_count = rounded.shape[2]
    modes_full = None
    left = jnp.transpose(rounded, (0, 2, 1)).reshape(clusters * mode_count, count)
    modes_full = jnp.dot(left, flat, preferred_element_type=jnp.float32)
    packed = modes_full.astype(jnp.bfloat16).reshape(clusters, mode_count, variables, cells)
    modes_out = lax.all_to_all(packed, "clus", split_axis=0, concat_axis=3, tiled=True)
    select = (successor[:, None] == cluster_ids[None, :]).astype(jnp.float32)
    wide = rounded.astype(jnp.float32)
    partner = jnp.einsum("ab,bsn->asn", select, wide, precision=lax.Precision.HIGHEST)
    image = jnp.einsum("st,atn->asn", gram, partner, precision=lax.Precision.HIGHEST)
    correlations = jnp.einsum("asm,asn->amn", wide, image, precision=lax.Precision.HIGHEST)
    own_correlation = lax.dynamic_slice_in_dim(correlations, owner, 1, 0)
    return (modes_out, coefficients, own_correlation)


def solution(mesh):
    in_specs = (P("groups", None, ("space", "clus")), P("groups"), P("groups", None), P("groups"))
    out_specs = (
        P(("groups", "clus"), None, None, "space"),
        P(("groups", "clus"), None),
        P(("groups", "clus"), None, None),
    )
    return jax.shard_map(local, mesh=mesh, in_specs=in_specs, out_specs=out_specs, check_vma=False)
```

profile of v0, /device:TPU:8, one launch (start us, length us, event | category | flops | bytes accessed | tf_op | source)
XLA Modules:
  0.0 174.2 jit_solution(173776694287602055)
XLA Ops:
  7.2 5.1 %convolution_bitcast_fusion = f32[128,128]{1,0:T(8,128)} fusion(bf16[128,5,3072]{2,0,1:T(8,128)(2,1)} %param.7), kind=kOutput, calls=%fused_computation.1 | convolution fusion | flops 503316480 | bytes 3997696 | tf_op jit(solution)/shard_map/dot_general | solution.py:31
  12.4 6.3 %copy.38 = bf16[128,5,3072]{0,2,1:T(8,128)(2,1)} copy(bf16[128,5,3072]{2,0,1:T(8,128)(2,1)} %param.7) | data formatting | bytes 7864320 | tf_op args[0]
  18.7 82.0 %all-reduce.2.cloned.1.call-done = f32[128,128]{1,0:T(8,128)} async-done(((f32[128,128]{1,0:T(8,128)}), f32[128,128]{1,0:T(8,128)}) %all-reduce.2.cloned.1.call-update) | async-done | bytes 65552 | tf_op jit(solution)/shard_map/psum | solution.py:34
  100.7 1.1 fusion.3
  101.8 0.2 fusion.35
  102.1 5.9 %custom-call.8 = f32[4,16,16]{2,1,0:T(8,128)S(1)} custom-call(f32[4,16,16]{2,1,0:T(8,128)S(1)} %fusion.16), custom_call_target="Cholesky" | custom-call | tf_op jit(solution)/shard_map/jit(cholesky)/cholesky | solution.py:18
  108.2 4.9 %custom-call.9 = f32[4,1,16,16]{2,3,1,0:T(8,128)S(1)} custom-call(f32[4,1,16,16]{3,2,1,0:T(8,128)S(1)} %select_bitcast_fusion.1), custom_call_target="InvertDiagBlocksLowerTriangular" | custom-call | tf_op jit(solution)/shard_map/triangular_solve/custom-call.0 | solution.py:19
  113.1 0.3 convolution_bitcast_fusion.1
  113.4 1.1 fusion.1
  114.5 0.2 fusion.36
  114.7 5.9 %custom-call.10 = f32[4,16,16]{2,1,0:T(8,128)S(1)} custom-call(f32[4,16,16]{2,1,0:T(8,128)S(1)} %fusion.14), custom_call_target="Cholesky" | custom-call | tf_op jit(solution)/shard_map/jit(cholesky)/cholesky | solution.py:18
  120.8 4.9 %custom-call.11 = f32[4,1,16,16]{2,3,1,0:T(8,128)S(1)} custom-call(f32[4,1,16,16]{3,2,1,0:T(8,128)S(1)} %select_bitcast_fusion), custom_call_target="InvertDiagBlocksLowerTriangular" | custom-call | tf_op jit(solution)/shard_map/triangular_solve/custom-call.0 | solution.py:19
  125.7 0.3 bitcast_convert_fusion
  126.0 4.9 %convolution_convert_fusion = bf16[64,15360]{1,0:T(8,128)(2,1)} fusion(bf16[64,128]{1,0:T(8,128)(2,1)S(1)} %bitcast.78, bf16[128,15360]{0,1:T(8,128)(2,1)} %bitcast.75), kind=kOutput, calls=%fused_computation | convolution fusion | flops 252641280 | bytes 5914624 | tf_op jit(solution)/shard_map/dot_general | solution.py:45
  130.9 4.6 %reshape.50 = bf16[4,16,5,3072]{3,2,1,0:T(8,128)(2,1)S(1)} reshape(bf16[64,15360]{1,0:T(8,128)(2,1)} %convolution_convert_fusion) | data formatting | bytes 3932160 | tf_op jit(solution)/shard_map/reshape | solution.py:46
  135.5 2.6 %copy.39 = bf16[4,16,5,3072]{3,1,2,0:T(8,128)(2,1)} copy(bf16[4,16,5,3072]{3,2,1,0:T(8,128)(2,1)S(1)} %reshape.50) | data formatting | bytes 3932160 | tf_op jit(solution)/shard_map/reshape | solution.py:46
  138.1 3.6 %all-to-all-start = ((bf16[4,16,5,3072]{3,1,2,0:T(8,128)(2,1)}), bf16[4,16,5,3072]{3,1,2,0:T(8,128)(2,1)S(1)}, u32[]{:S(2)}, u32[]{:S(2)}) async-start(bf16[4,16,5,3072]{3,1,2,0:T(8,128)(2,1)} %copy.39), calls=%async_computation | async-start | bytes 3932160 | tf_op jit(solution)/shard_map/all_to_all | solution.py:47
  141.7 0.7 constant_dynamic-slice_fusion.1
  142.4 0.2 fusion.22
  142.6 0.2 fusion.4
  142.8 0.1 fusion.37
  143.0 0.6 constant_dynamic-slice_fusion
  143.6 22.4 %all-to-all-done = bf16[4,16,5,3072]{3,1,2,0:T(8,128)(2,1)S(1)} async-done(((bf16[4,16,5,3072]{3,1,2,0:T(8,128)(2,1)}), bf16[4,16,5,3072]{3,1,2,0:T(8,128)(2,1)S(1)}, u32[]{:S(2)}, u32[]{:S(2)}) %all-to-all-start) | async-done | bytes 1966112 | tf_op jit(solution)/shard_map/all_to_all | solution.py:47
  165.9 1.4 copy.52
  (24 shorter events, 0.7 us)
Async XLA Ops:
  7.2 5.2 %copy-start.2 = (s32[128]{0:T(128)S(1)}, s32[128]{0:T(128)}, u32[]{:S(2)}) copy-start(s32[128]{0:T(128)} %param.8) | copy-start | bytes 1540
  7.2 93.5 %all-reduce.2.cloned.1.call-start = ((), (), s32[]{:S(2)}) async-start(), calls=%async_computation.1 | async-start | bytes 131072 | tf_op jit(solution)/shard_map/psum | solution.py:34
  12.4 88.3 %copy-start.1 = (f32[128,16]{0,1:T(8,128)S(1)}, f32[128,16]{0,1:T(8,128)}, u32[]{:S(2)}) copy-start(f32[128,16]{0,1:T(8,128)} %param.9) | copy-start | bytes 24580
  135.5 6.9 %copy-start.3 = (s32[4]{0:T(128)S(1)}, s32[4]{0:T(128)}, u32[]{:S(2)}) copy-start(s32[4]{0:T(128)} %param.10) | copy-start | bytes 52
  135.5 7.1 %copy-start = (f32[128,128]{1,0:T(8,128)S(1)}, f32[128,128]{1,0:T(8,128)}, u32[]{:S(2)}) copy-start(f32[128,128]{1,0:T(8,128)} %all-reduce.2.cloned.1.call-done) | copy-start | bytes 196612
  138.1 27.9 %all-to-all-start = ((bf16[4,16,5,3072]{3,1,2,0:T(8,128)(2,1)}), bf16[4,16,5,3072]{3,1,2,0:T(8,128)(2,1)S(1)}, u32[]{:S(2)}, u32[]{:S(2)}) async-start(bf16[4,16,5,3072]{3,1,2,0:T(8,128)(2,1)} %copy.39), calls=%async_computation | async-start | bytes 3932160 | tf_op jit(solution)/shard_map/all_to_all | solution.py:47
Sparse Core Ops, SparseCore 0:
  12.5 88.1 all-reduce.1
where the time goes:
time: 175 us; the launch traced here: 174 us
  waiting for transfers between devices  104 us (59%)
  other arithmetic  22.1 us (13%)
  local copies, waits for them, and re-layouts  16.3 us (9%)
  between operations  14.2 us (8%)
  matrix products  13.6 us (8%)
  starting transfers between devices  3.64 us (2%)
    psum x1, waiting for transfers between devices, local(): gram = lax.psum(partial_value, ('space', 'clus')) / total_rows  82 us
    all_to_all x1, waiting for transfers between devices, local(): lax.all_to_all(packed, 'clus', split_axis=0, concat_axis=3, tiled=True)  22.4 us
    another operation x7, other arithmetic, subspace(): lower = jnp.linalg.cholesky(inner)  12 us
    another operation x5, other arithmetic, subspace(): lax.linalg.triangular_solve(lower, image, left_side=False, lower=True, tr...  9.99 us
    reshape x2, local copies, waits for them, and re-layouts, local(): modes_full.astype(jnp.bfloat16)  7.12 us
    unnamed x9, local copies, waits for them, and re-layouts  6.29 us
    dot_general x1, matrix products, local(): lax.dot_general(flat, flat, (((1,), (1,)), ((), ())), preferred_element_t...  5.13 us
    dot_general x1, matrix products, local(): modes_full = jnp.dot(left, flat, preferred_element_type=jnp.float32)  4.86 us
  transfers between devices with their start and end apart: 2, of which 2 were waited for; matrix products, arithmetic and copies ran while one was open for 5% of the time, Pallas kernels for 0%

commit v1 on v0

--- a/solution.py
+++ b/solution.py
@@ -31,7 +31,7 @@
     partial_value = lax.dot_general(
         flat, flat, (((1,), (1,)), ((), ())), preferred_element_type=jnp.float32
     )
-    gram = lax.psum(partial_value, ("space", "clus")) / total_rows
+    gram = jnp.sum(lax.all_gather(partial_value, ("space", "clus")), axis=0) / total_rows
     cluster_ids = jnp.arange(clusters, dtype=jnp.int32)
     member = (labels[None, :] == cluster_ids[:, None]).astype(jnp.float32)
     basis = subspace(gram, member, start)

time: 175 us -> 127 us (0.73)
  the two profiles are of different devices: /device:TPU:8 before, /device:TPU:0 now
where the time goes in v1:
time: 127 us; the launch traced here: 126 us
  waiting for transfers between devices  56.8 us (45%)
  other arithmetic  23.3 us (18%)
  local copies, waits for them, and re-layouts  16.3 us (13%)
  between operations  14.2 us (11%)
  matrix products  12 us (9%)
  starting transfers between devices  3.64 us (3%)
    all_gather x1, waiting for transfers between devices, local(): lax.all_gather(partial_value, ('space', 'clus'))  34.4 us
    all_to_all x1, waiting for transfers between devices, local(): lax.all_to_all(packed, 'clus', split_axis=0, concat_axis=3, tiled=True)  22.4 us
    another operation x7, other arithmetic, subspace(): lower = jnp.linalg.cholesky(inner)  12 us
    another operation x5, other arithmetic, subspace(): lax.linalg.triangular_solve(lower, image, left_side=False, lower=True, tr...  9.99 us
    reshape x2, local copies, waits for them, and re-layouts, local(): modes_full.astype(jnp.bfloat16)  7.12 us
    unnamed x7, local copies, waits for them, and re-layouts  6.29 us
    dot_general x1, matrix products, local(): lax.dot_general(flat, flat, (((1,), (1,)), ((), ())), preferred_element_t...  5.13 us
    dot_general x1, matrix products, local(): modes_full = jnp.dot(left, flat, preferred_element_type=jnp.float32)  4.86 us
  transfers between devices with their start and end apart: 2, of which 2 were waited for; matrix products, arithmetic and copies ran while one was open for 6% of the time, Pallas kernels for 0%

profile of v1, /device:TPU:0, one launch (start us, length us, event | category | flops | bytes accessed | tf_op | source)
XLA Modules:
  0.0 126.3 jit_solution(17681398155355237147)
XLA Ops:
  7.2 5.1 %convolution_bitcast_fusion = f32[128,128]{1,0:T(8,128)} fusion(bf16[128,5,3072]{2,0,1:T(8,128)(2,1)} %param.7), kind=kOutput, calls=%fused_computation.1 | convolution fusion | flops 503316480 | bytes 3997696 | tf_op jit(solution)/shard_map/dot_general | solution.py:31
  12.4 6.3 %copy.38 = bf16[128,5,3072]{0,2,1:T(8,128)(2,1)} copy(bf16[128,5,3072]{2,0,1:T(8,128)(2,1)} %param.7) | data formatting | bytes 7864320 | tf_op args[0]
  18.7 34.4 %all-gather.3.cloned.1.call-done = f32[2048,128]{1,0:T(8,128)} async-done(((f32[128,128]{1,0:T(8,128)}), f32[2048,128]{1,0:T(8,128)}) %all-gather.3.cloned.1.call-update) | async-done | bytes 1048592 | tf_op jit(solution)/shard_map/all_gather | solution.py:34
  53.1 1.3 %reduce_sum.9 = f32[128,128]{1,0:T(8,128)S(1)} reduce(f32[16,128,128]{2,1,0:T(8,128)} %bitcast.79, f32[]{:T(128)} %constant.40.clone.1), dimensions={0}, to_apply=%region_0.0 | reduce | flops 245760 | bytes 1114116 | tf_op jit(solution)/shard_map/reduce_sum | solution.py:34
  54.4 0.2 fusion.3
  54.7 0.2 fusion.35
  55.0 5.9 %custom-call.8 = f32[4,16,16]{2,1,0:T(8,128)S(1)} custom-call(f32[4,16,16]{2,1,0:T(8,128)S(1)} %fusion.16), custom_call_target="Cholesky" | custom-call | tf_op jit(solution)/shard_map/jit(cholesky)/cholesky | solution.py:18
  61.1 4.9 %custom-call.9 = f32[4,1,16,16]{2,3,1,0:T(8,128)S(1)} custom-call(f32[4,1,16,16]{3,2,1,0:T(8,128)S(1)} %select_bitcast_fusion.1), custom_call_target="InvertDiagBlocksLowerTriangular" | custom-call | tf_op jit(solution)/shard_map/triangular_solve/custom-call.0 | solution.py:19
  66.0 0.3 convolution_bitcast_fusion.1
  66.3 0.2 fusion.1
  66.5 0.2 fusion.36
  66.8 5.9 %custom-call.10 = f32[4,16,16]{2,1,0:T(8,128)S(1)} custom-call(f32[4,16,16]{2,1,0:T(8,128)S(1)} %fusion.14), custom_call_target="Cholesky" | custom-call | tf_op jit(solution)/shard_map/jit(cholesky)/cholesky | solution.py:18
  72.9 4.9 %custom-call.11 = f32[4,1,16,16]{2,3,1,0:T(8,128)S(1)} custom-call(f32[4,1,16,16]{3,2,1,0:T(8,128)S(1)} %select_bitcast_fusion), custom_call_target="InvertDiagBlocksLowerTriangular" | custom-call | tf_op jit(solution)/shard_map/triangular_solve/custom-call.0 | solution.py:19
  77.8 0.3 bitcast_convert_fusion
  78.1 4.9 %convolution_convert_fusion = bf16[64,15360]{1,0:T(8,128)(2,1)} fusion(bf16[64,128]{1,0:T(8,128)(2,1)S(1)} %bitcast.80, bf16[128,15360]{0,1:T(8,128)(2,1)} %bitcast.76), kind=kOutput, calls=%fused_computation | convolution fusion | flops 252641280 | bytes 5914624 | tf_op jit(solution)/shard_map/dot_general | solution.py:45
  83.0 4.6 %reshape.50 = bf16[4,16,5,3072]{3,2,1,0:T(8,128)(2,1)S(1)} reshape(bf16[64,15360]{1,0:T(8,128)(2,1)} %convolution_convert_fusion) | data formatting | bytes 3932160 | tf_op jit(solution)/shard_map/reshape | solution.py:46
  87.5 2.6 %copy.39 = bf16[4,16,5,3072]{3,1,2,0:T(8,128)(2,1)} copy(bf16[4,16,5,3072]{3,2,1,0:T(8,128)(2,1)S(1)} %reshape.50) | data formatting | bytes 3932160 | tf_op jit(solution)/shard_map/reshape | solution.py:46
  90.1 3.6 %all-to-all-start = ((bf16[4,16,5,3072]{3,1,2,0:T(8,128)(2,1)}), bf16[4,16,5,3072]{3,1,2,0:T(8,128)(2,1)S(1)}, u32[]{:S(2)}, u32[]{:S(2)}) async-start(bf16[4,16,5,3072]{3,1,2,0:T(8,128)(2,1)} %copy.39), calls=%async_computation | async-start | bytes 3932160 | tf_op jit(solution)/shard_map/all_to_all | solution.py:47
  93.7 0.7 constant_dynamic-slice_fusion.1
  94.4 0.2 fusion.22
  94.6 0.2 fusion.4
  95.0 0.6 constant_dynamic-slice_fusion
  95.6 22.4 %all-to-all-done = bf16[4,16,5,3072]{3,1,2,0:T(8,128)(2,1)S(1)} async-done(((bf16[4,16,5,3072]{3,1,2,0:T(8,128)(2,1)}), bf16[4,16,5,3072]{3,1,2,0:T(8,128)(2,1)S(1)}, u32[]{:S(2)}, u32[]{:S(2)}) %all-to-all-start) | async-done | bytes 1966112 | tf_op jit(solution)/shard_map/all_to_all | solution.py:47
  118.0 1.4 %copy.52 = bf16[1,4,5,2,8,3072]{5,4,1,3,2,0:T(8,128)(2,1)} copy(bf16[1,4,5,2,8,3072]{5,4,3,2,1,0:T(8,128)(2,1)S(1)} %bitcast.77) | data formatting | bytes 3932160 | tf_op jit(solution)/shard_map/all_to_all | solution.py:47
  (23 shorter events, 0.9 us)
Async XLA Ops:
  7.2 46.0 %all-gather.3.cloned.1.call-start = ((), (), s32[]{:S(2)}) async-start(), calls=%async_computation.1 | async-start | bytes 1114112 | tf_op jit(solution)/shard_map/all_gather | solution.py:34
  12.4 6.3 %copy-start.1 = (s32[128]{0:T(128)S(1)}, s32[128]{0:T(128)}, u32[]{:S(2)}) copy-start(s32[128]{0:T(128)} %param.8) | copy-start | bytes 1540
  12.4 42.1 %copy-start = (f32[128,16]{0,1:T(8,128)S(1)}, f32[128,16]{0,1:T(8,128)}, u32[]{:S(2)}) copy-start(f32[128,16]{0,1:T(8,128)} %param.9) | copy-start | bytes 24580
  87.5 6.9 %copy-start.2 = (s32[4]{0:T(128)S(1)}, s32[4]{0:T(128)}, u32[]{:S(2)}) copy-start(s32[4]{0:T(128)} %param.10) | copy-start | bytes 52
  90.1 27.9 %all-to-all-start = ((bf16[4,16,5,3072]{3,1,2,0:T(8,128)(2,1)}), bf16[4,16,5,3072]{3,1,2,0:T(8,128)(2,1)S(1)}, u32[]{:S(2)}, u32[]{:S(2)}) async-start(bf16[4,16,5,3072]{3,1,2,0:T(8,128)(2,1)} %copy.39), calls=%async_computation | async-start | bytes 3932160 | tf_op jit(solution)/shard_map/all_to_all | solution.py:47
Sparse Core Ops, SparseCore 0:
  12.5 40.6 all-gather.2
